TPU v7x, 32 devices: a whole 2x2x4 slice. The times are simulated.
32 devices in a mesh: prow: 8 (over z, core), pcol: 4 (over y, x).
Axes of the slice: x: 2, y: 2, z: 4, core: 2. Of those that a mesh axis runs over, the one named last changes fastest.
Arguments:
- leaf_source: bfloat16 [8, 4, 8, 256, 128], P('prow', 'pcol'), may hold values from -6 to 6
- band_source: bfloat16 [8, 256, 128], P('prow'), may hold values from -6 to 6
- strip_source: bfloat16 [4, 256, 128], P('pcol'), may hold values from -6 to 6
- summit_source: bfloat16 [256, 128], replicated, may hold values from -6 to 6
- leaf_inverse: bfloat16 [8, 4, 8, 256, 256], P('prow', 'pcol'), may hold values from -1 to 2
- band_inverse: bfloat16 [8, 256, 256], P('prow'), may hold values from -1 to 2
- strip_inverse: bfloat16 [4, 256, 256], P('pcol'), may hold values from -1 to 2
- summit_inverse: bfloat16 [256, 256], replicated, may hold values from -1 to 2
- leaf_blocks: bfloat16 [8, 4, 28, 256, 256], P('prow', 'pcol'), may hold values from -0.09375 to 0.09375
- band_blocks: bfloat16 [8, 4, 8, 256, 256], P('prow', 'pcol'), may hold values from -0.046875 to 0.046875
- strip_blocks: bfloat16 [8, 4, 8, 256, 256], P('prow', 'pcol'), may hold values from -0.03125 to 0.03125
- summit_blocks: bfloat16 [8, 4, 8, 256, 256], P('prow', 'pcol'), may hold values from -0.046875 to 0.046875
- coupling: bfloat16 [8, 4, 256, 256], P('prow', 'pcol'), may hold values from -0.09375 to 0.09375
- summit_band: bfloat16 [8, 256, 256], P('prow', 'pcol'), may hold values from -0.078125 to 0.078125
- summit_strip: bfloat16 [4, 256, 256], P('pcol'), may hold values from -0.078125 to 0.078125
- parents: int32 [8, 4, 8], P('prow', 'pcol'), may hold values from 1 to 8, as said below
- widths: int32 [8, 4, 8], P('prow', 'pcol'), may hold values from 64 to 256
Outputs:
- leaf_answer: bfloat16 [8, 4, 8, 256, 128], P('prow', 'pcol')
- band_answer: bfloat16 [8, 256, 128], P('prow')
- strip_answer: bfloat16 [4, 256, 128], P('pcol')
- summit_answer: bfloat16 [256, 128], replicated
Inputs may be any that keep to these rules, and one draw needn't show every extreme that they name: parents[r, c, a] is a later leaf of the same subtree, or 8 where leaf a links only to the separators.
All inputs are finite; a program needn't handle non-finite values.
Results may differ from a plain program's by a relative error of at most 0.015.
Values sent between devices are 32-bit elements; how exact they have to be, the bound alone decides.
No kernel may reach another device: no remote copies, remote signals or barrier semaphores. Data moves between devices by JAX's collectives and lax.ppermute only.
A program may use at most 64 MiB of HBM per device.

v0:
```python
import jax
import jax.numpy as jnp
from jax import lax
from jax.sharding import PartitionSpec as P

PASSES = 2


def ancestors(parent_list, leaf_count):
    node_ids = jnp.arange(leaf_count + 1, dtype=jnp.int32)
    current = parent_list
    extended = jnp.concatenate([current, jnp.full((1,), leaf_count, jnp.int32)])
    reached = jnp.zeros((leaf_count + 1, leaf_count), jnp.float32)
    for repeat in range(leaf_count):
        matches = current[None, :] == node_ids[:, None]
        reached = jnp.maximum(reached, matches.astype(jnp.float32))
        current = jnp.sum(jnp.where(matches, extended[:, None], 0), axis=0)
    return reached[:leaf_count]


def multiply(left, right, form):
    return jnp.einsum(form, left, right, preferred_element_type=jnp.float32)


def forward_block(inverse, source, partial_value):
    residual = (source.astype(jnp.float32) - partial_value).astype(jnp.bfloat16)
    return multiply(inverse, residual, "ij,jr->ir").astype(jnp.bfloat16)


def backward_block(inverse, source, partial_value):
    residual = (source.astype(jnp.float32) - partial_value).astype(jnp.bfloat16)
    return multiply(inverse, residual, "ji,jr->ir").astype(jnp.bfloat16)


def leaf_forward(pair_blocks, inverses, sources, reached, row_mask):
    leaf_count = sources.shape[0]
    solved = []
    for position in range(leaf_count):
        residual = sources[position].astype(jnp.float32)
        if position > 0:
            first_pair = position * (position - 1) // 2
            weights = reached[position, :position].astype(jnp.bfloat16)
            stacked = jnp.stack(solved) * weights[:, None, None]
            residual = residual - multiply(
                pair_blocks[first_pair : first_pair + position], stacked, "bij,bjr->ir"
            )
        residual = (row_mask[position] * residual).astype(jnp.bfloat16)
        solved.append(
            (row_mask[position] * multiply(inverses[position], residual, "ij,jr->ir")).astype(
                jnp.bfloat16
            )
        )
    return jnp.stack(solved)


def leaf_backward(pair_blocks, inverses, solved, outer, reached, row_mask):
    leaf_count = solved.shape[0]
    pending = outer
    answers = [None] * leaf_count
    for position in reversed(range(leaf_count)):
        residual = (
            row_mask[position] * (solved[position].astype(jnp.float32) - pending[position])
        ).astype(jnp.bfloat16)
        update = (row_mask[position] * multiply(inverses[position], residual, "ji,jr->ir")).astype(
            jnp.bfloat16
        )
        answers[position] = update
        if position > 0:
            first_pair = position * (position - 1) // 2
            pushed = multiply(
                pair_blocks[first_pair : first_pair + position], update, "bji,jr->bir"
            )
            pending = pending.at[:position].add(
                reached[position, :position][:, None, None] * pushed
            )
    return jnp.stack(answers)


def per_device(
    leaf_source,
    band_source,
    strip_source,
    summit_source,
    leaf_inverse,
    band_inverse,
    strip_inverse,
    summit_inverse,
    leaf_blocks,
    band_blocks,
    strip_blocks,
    summit_blocks,
    coupling,
    summit_band,
    summit_strip,
    parents,
    widths,
):
    leaf_count = leaf_source.shape[2]
    block_width = leaf_source.shape[3]
    reached = ancestors(parents[0, 0], leaf_count)
    column_ids = jnp.arange(block_width, dtype=jnp.int32)
    row_mask = (column_ids[None, :] < widths[0, 0][:, None]).astype(jnp.float32)[:, :, None]
    band_slab = summit_band.shape[1]
    column_place = lax.axis_index("pcol") * band_slab
    inverses = leaf_inverse[0, 0]
    pair_blocks = leaf_blocks[0, 0]
    to_band = band_blocks[0, 0]
    to_strip = strip_blocks[0, 0]
    to_summit = summit_blocks[0, 0]
    link_block = coupling[0, 0]
    lift_band = summit_band[0]
    lift_strip = summit_strip[0]
    current = (leaf_source[0, 0], band_source[0], strip_source[0], summit_source)
    for iteration in range(PASSES):
        leaf_now, band_now, strip_now, summit_now = current
        solved = leaf_forward(pair_blocks, inverses, leaf_now, reached, row_mask)
        band_term = multiply(to_band, solved, "aij,ajr->ir")
        strip_term = multiply(to_strip, solved, "aij,ajr->ir")
        summit_term = multiply(to_summit, solved, "aij,ajr->ir")
        band_partial = lax.psum(band_term, "pcol")
        band_solved = forward_block(band_inverse[0], band_now, band_partial)
        own_band = lax.dynamic_slice_in_dim(band_solved, column_place, band_slab, 0)
        summit_term = summit_term + multiply(lift_band, own_band, "ki,kn->in")
        strip_term = strip_term + multiply(link_block, band_solved, "ij,jn->in")
        strip_partial, summit_early = lax.psum((strip_term, summit_term), "prow")
        strip_solved = forward_block(strip_inverse[0], strip_now, strip_partial)
        summit_partial = lax.psum(
            summit_early + multiply(lift_strip, strip_solved, "ki,kn->in"), "pcol"
        )
        summit_solved = forward_block(summit_inverse, summit_now, summit_partial)
        summit_answer = backward_block(
            summit_inverse, summit_solved, jnp.zeros(summit_solved.shape, jnp.float32)
        )
        strip_answer = backward_block(
            strip_inverse[0], strip_solved, multiply(lift_strip, summit_answer, "ki,in->kn")
        )
        downward = multiply(link_block, strip_answer, "ji,jn->in")
        band_piece = multiply(lift_band, summit_answer, "ki,in->kn")
        band_back = lax.psum(downward, "pcol") + lax.all_gather(
            band_piece, "pcol", axis=0, tiled=True
        )
        band_answer = backward_block(band_inverse[0], band_solved, band_back)
        outer = (
            multiply(to_band, band_answer, "aij,ir->ajr")
            + multiply(to_strip, strip_answer, "aij,ir->ajr")
            + multiply(to_summit, summit_answer, "aij,ir->ajr")
        )
        leaf_answer = leaf_backward(pair_blocks, inverses, solved, outer, reached, row_mask)
        current = (leaf_answer, band_answer, strip_answer, summit_answer)
    return (current[0][None, None], current[1][None], current[2][None], current[3])


def solution(mesh):
    placed = (
        P("prow", "pcol", None, None, None),
        P("prow", None, None),
        P("pcol", None, None),
        P(),
        P("prow", "pcol", None, None, None),
        P("prow", None, None),
        P("pcol", None, None),
        P(),
        P("prow", "pcol", None, None, None),
        P("prow", "pcol", None, None, None),
        P("prow", "pcol", None, None, None),
        P("prow", "pcol", None, None, None),
        P("prow", "pcol", None, None),
        P("prow", "pcol", None),
        P("pcol", None, None),
        P("prow", "pcol", None),
        P("prow", "pcol", None),
    )
    return jax.shard_map(
        per_device,
        mesh=mesh,
        in_specs=placed,
        out_specs=(
            P("prow", "pcol", None, None, None),
            P("prow", None, None),
            P("pcol", None, None),
            P(),
        ),
        check_vma=False,
    )
```

profile of v0, /device:TPU:0, one launch (start us, length us, event | category | flops | bytes accessed | tf_op | source)
XLA Modules:
  0.0 482.1 jit_solution(6182447190945887679)
XLA Ops:
  13.9 1.9 constant_dynamic-update-slice_fusion.17
  15.8 2.0 constant_dynamic-update-slice_fusion.16
  17.8 2.1 constant_dynamic-update-slice_fusion.15
  19.8 2.1 constant_dynamic-update-slice_fusion.14
  21.9 2.2 constant_dynamic-update-slice_fusion.13
  25.1 2.5 constant_dynamic-update-slice_fusion.12
  28.4 2.6 constant_dynamic-update-slice_fusion.11
  31.0 2.6 constant_dynamic-update-slice_fusion.18
  33.6 2.2 convolution_bitcast_fusion.21
  35.9 1.3 slice_bitcast_fusion.14
  37.2 1.2 slice_bitcast_fusion.15
  38.4 1.2 slice_bitcast_fusion.16
  39.6 1.2 slice_bitcast_fusion.17
  40.8 2.1 convolution_bitcast_fusion.19
  43.0 2.1 convolution_bitcast_fusion.20
  45.1 35.8 %all-reduce.11.cloned.1.call-done = f32[256,128]{1,0:T(8,128)} async-done(((f32[256,128]{1,0:T(8,128)}), f32[256,128]{1,0:T(8,128)}) %all-reduce.11.cloned.1.call-update) | async-done | bytes 131088 | tf_op jit(solution)/shard_map/psum | solution.py:120
  80.9 1.2 convolution_convert_fusion.11
  82.1 1.8 fusion.31
  83.9 1.8 fusion.36
  85.8 1.3 slice_bitcast_fusion.18
  87.1 54.4 %all-reduce.25.cloned.1.call-done = (f32[256,128]{1,0:T(8,128)}, f32[256,128]{1,0:T(8,128)}) async-done(((f32[256,128]{1,0:T(8,128)}, f32[256,128]{1,0:T(8,128)}), (f32[256,128]{1,0:T(8,128)}, f32[256,128]{1,0:T(8,128)})) %all-reduce.25.cloned.1.call-update) | async-done | bytes 262160 | tf_op jit(solution)/shard_map/psum | solution.py:125
  141.5 1.1 convolution_convert_fusion.10
  143.2 1.8 fusion.30
  145.1 1.2 slice_bitcast_fusion.19
  146.3 40.2 %all-reduce.13.cloned.1.call-done = f32[256,128]{1,0:T(8,128)} async-done(((f32[256,128]{1,0:T(8,128)}), f32[256,128]{1,0:T(8,128)}) %all-reduce.13.cloned.1.call-update) | async-done | bytes 131088 | tf_op jit(solution)/shard_map/psum | solution.py:127
  186.5 2.0 convolution_convert_fusion.8
  188.5 1.8 convolution_convert_fusion.7
  190.3 1.7 convolution_bitcast_fusion.11
  193.0 9.1 %all_gather.6 = f32[256,128]{1,0:T(8,128)} all-gather(f32[64,128]{1,0:T(8,128)S(1)} %convolution_bitcast_fusion.24), channel_id=1, replica_groups=mesh['prow'=8,'pcol'=4] {'pcol'}, dimensions={0}, use_global_device_ids=true | all-gather | bytes 163840 | tf_op jit(solution)/shard_map/all_gather | solution.py:139
  202.1 1.7 copy.39
  203.8 30.6 %all-reduce.15.cloned.1.call-done = f32[256,128]{0,1:T(8,128)} async-done(((f32[256,128]{0,1:T(8,128)}), f32[256,128]{0,1:T(8,128)}) %all-reduce.15.cloned.1.call-update) | async-done | bytes 131088 | tf_op jit(solution)/shard_map/psum | solution.py:139
  234.4 1.2 convolution_convert_fusion.6
  236.6 1.3 convolution_add_fusion.3
  243.1 1.4 fusion.79
  244.6 2.0 constant_dynamic-update-slice_fusion.43
  246.6 2.1 constant_dynamic-update-slice_fusion.42
  248.7 2.2 constant_dynamic-update-slice_fusion.41
  250.9 2.3 constant_dynamic-update-slice_fusion.40
  253.2 2.4 constant_dynamic-update-slice_fusion.39
  255.6 2.5 constant_dynamic-update-slice_fusion.38
  258.1 2.6 constant_dynamic-update-slice_fusion.37
  260.7 2.7 constant_dynamic-update-slice_fusion.44
  263.4 2.2 convolution_bitcast_fusion.15
  265.6 2.2 convolution_bitcast_fusion.17
  267.9 2.2 convolution_bitcast_fusion.16
  270.0 40.1 %all-reduce.17.cloned.1.call-done = f32[256,128]{0,1:T(8,128)} async-done(((f32[256,128]{0,1:T(8,128)}), f32[256,128]{0,1:T(8,128)}) %all-reduce.17.cloned.1.call-update) | async-done | bytes 131088 | tf_op jit(solution)/shard_map/psum | solution.py:120
  310.2 1.2 convolution_convert_fusion.5
  311.4 1.8 fusion.35
  313.2 1.8 fusion.28
  315.1 55.6 %all-reduce.23.cloned.1.call-done = (f32[256,128]{0,1:T(8,128)}, f32[256,128]{0,1:T(8,128)}) async-done(((f32[256,128]{0,1:T(8,128)}, f32[256,128]{0,1:T(8,128)}), (f32[256,128]{0,1:T(8,128)}, f32[256,128]{0,1:T(8,128)})) %all-reduce.23.cloned.1.call-update) | async-done | bytes 262160 | tf_op jit(solution)/shard_map/psum | solution.py:125
  370.7 1.1 convolution_convert_fusion.4
  372.4 1.7 fusion.27
  374.2 41.4 %all-reduce.19.cloned.1.call-done = f32[256,128]{0,1:T(8,128)} async-done(((f32[256,128]{0,1:T(8,128)}), f32[256,128]{0,1:T(8,128)}) %all-reduce.19.cloned.1.call-update) | async-done | bytes 131088 | tf_op jit(solution)/shard_map/psum | solution.py:127
  415.6 2.0 convolution_convert_fusion.2
  417.6 1.8 convolution_convert_fusion.1
  419.5 1.7 convolution_bitcast_fusion.8
  422.2 1.6 copy.44
  423.8 1.6 copy.43
  425.4 8.8 %all_gather.7 = f32[256,128]{1,0:T(8,128)S(1)} all-gather(f32[64,128]{1,0:T(8,128)S(1)} %convolution_bitcast_fusion.23), channel_id=1, replica_groups=mesh['prow'=8,'pcol'=4] {'pcol'}, dimensions={0}, use_global_device_ids=true | all-gather | bytes 163840 | tf_op jit(solution)/shard_map/all_gather | solution.py:139
  434.2 29.4 %all-reduce.21.cloned.1.call-done = f32[256,128]{0,1:T(8,128)} async-done(((f32[256,128]{0,1:T(8,128)}), f32[256,128]{0,1:T(8,128)}) %all-reduce.21.cloned.1.call-update) | async-done | bytes 131088 | tf_op jit(solution)/shard_map/psum | solution.py:139
  463.6 1.2 convolution_convert_fusion
  464.8 1.3 fusion.132
  466.8 1.7 convolution_add_fusion.1
  472.3 1.9 fusion.123
  (241 shorter events, 22.3 us)
Async XLA Ops:
  7.2 26.5 %copy-start = (bf16[1,1,8,256,256]{4,3,2,1,0:T(8,128)(2,1)S(1)}, bf16[1,1,8,256,256]{4,3,2,1,0:T(8,128)(2,1)}, u32[]{:S(2)}) copy-start(bf16[1,1,8,256,256]{4,3,2,1,0:T(8,128)(2,1)} %param.54) | copy-start | bytes 3145732
  7.2 73.7 %all-reduce.11.cloned.1.call-start = ((), (), s32[]{:S(2)}) async-start(), calls=%async_computation | async-start | bytes 262144 | tf_op jit(solution)/shard_map/psum | solution.py:120
  10.5 20.5 %copy-start.73 = (bf16[7]{0:T(256)(128)(2,1)}, bf16[7]{0:T(256)(128)(2,1)S(1)}, u32[]{:S(2)}) copy-start(bf16[7]{0:T(256)(128)(2,1)S(1)} %fusion.586) | copy-start | bytes 46
  10.5 17.8 %copy-start.74 = (bf16[6]{0:T(256)(128)(2,1)}, bf16[6]{0:T(256)(128)(2,1)S(1)}, u32[]{:S(2)}) copy-start(bf16[6]{0:T(256)(128)(2,1)S(1)} %fusion.585) | copy-start | bytes 40
  10.6 14.5 %copy-start.75 = (bf16[5]{0:T(256)(128)(2,1)}, bf16[5]{0:T(256)(128)(2,1)S(1)}, u32[]{:S(2)}) copy-start(bf16[5]{0:T(256)(128)(2,1)S(1)} %fusion.584) | copy-start | bytes 34
  10.6 13.6 %copy-start.76 = (bf16[4]{0:T(256)(128)(2,1)}, bf16[4]{0:T(256)(128)(2,1)S(1)}, u32[]{:S(2)}) copy-start(bf16[4]{0:T(256)(128)(2,1)S(1)} %fusion.583) | copy-start | bytes 28
  10.6 13.5 %copy-start.77 = (bf16[3]{0:T(256)(128)(2,1)}, bf16[3]{0:T(256)(128)(2,1)S(1)}, u32[]{:S(2)}) copy-start(bf16[3]{0:T(256)(128)(2,1)S(1)} %fusion.582) | copy-start | bytes 22
  10.6 13.5 %copy-start.78 = (bf16[2]{0:T(256)(128)(2,1)}, bf16[2]{0:T(256)(128)(2,1)S(1)}, u32[]{:S(2)}) copy-start(bf16[2]{0:T(256)(128)(2,1)S(1)} %fusion.581) | copy-start | bytes 16
  12.0 12.1 %copy-start.55 = (f32[1,256]{1,0:T(1,128)}, f32[1,256]{1,0:T(1,128)S(1)}, u32[]{:S(2)}) copy-start(f32[1,256]{1,0:T(1,128)S(1)} %get-tuple-element.248) | copy-start | bytes 3076
  12.0 13.1 %copy-start.45 = (f32[1,256]{1,0:T(1,128)}, f32[1,256]{1,0:T(1,128)S(1)}, u32[]{:S(2)}) copy-start(f32[1,256]{1,0:T(1,128)S(1)} %get-tuple-element.243) | copy-start | bytes 3076
  12.1 16.3 %copy-start.48 = (f32[1,256]{1,0:T(1,128)}, f32[1,256]{1,0:T(1,128)S(1)}, u32[]{:S(2)}) copy-start(f32[1,256]{1,0:T(1,128)S(1)} %get-tuple-element.242) | copy-start | bytes 3076
  12.1 18.9 %copy-start.51 = (f32[1,256]{1,0:T(1,128)}, f32[1,256]{1,0:T(1,128)S(1)}, u32[]{:S(2)}) copy-start(f32[1,256]{1,0:T(1,128)S(1)} %get-tuple-element.241) | copy-start | bytes 3076
  15.8 11.8 %copy-start.26 = (bf16[128,256]{1,0:T(8,128)(2,1)}, bf16[128,256]{1,0:T(8,128)(2,1)S(1)}, u32[]{:S(2)}) copy-start(bf16[128,256]{1,0:T(8,128)(2,1)S(1)} %get-tuple-element.249) | copy-start | bytes 196612
  17.8 9.8 %copy-start.29 = (bf16[128,256]{1,0:T(8,128)(2,1)}, bf16[128,256]{1,0:T(8,128)(2,1)S(1)}, u32[]{:S(2)}) copy-start(bf16[128,256]{1,0:T(8,128)(2,1)S(1)} %get-tuple-element.250) | copy-start | bytes 196612
  19.8 7.8 %copy-start.31 = (bf16[128,256]{1,0:T(8,128)(2,1)}, bf16[128,256]{1,0:T(8,128)(2,1)S(1)}, u32[]{:S(2)}) copy-start(bf16[128,256]{1,0:T(8,128)(2,1)S(1)} %get-tuple-element.251) | copy-start | bytes 196612
  21.9 5.7 %copy-start.34 = (bf16[128,256]{1,0:T(8,128)(2,1)}, bf16[128,256]{1,0:T(8,128)(2,1)S(1)}, u32[]{:S(2)}) copy-start(bf16[128,256]{1,0:T(8,128)(2,1)S(1)} %get-tuple-element.252) | copy-start | bytes 196612
  25.1 15.7 %copy-start.2 = (bf16[1,1,8,256,256]{4,3,2,1,0:T(8,128)(2,1)S(1)}, bf16[1,1,8,256,256]{4,3,2,1,0:T(8,128)(2,1)}, u32[]{:S(2)}) copy-start(bf16[1,1,8,256,256]{4,3,2,1,0:T(8,128)(2,1)} %param.56) | copy-start | bytes 3145732
  28.4 14.6 %copy-start.1 = (bf16[1,1,8,256,256]{4,3,2,1,0:T(8,128)(2,1)S(1)}, bf16[1,1,8,256,256]{4,3,2,1,0:T(8,128)(2,1)}, u32[]{:S(2)}) copy-start(bf16[1,1,8,256,256]{4,3,2,1,0:T(8,128)(2,1)} %param.55) | copy-start | bytes 3145732
  31.0 51.1 %copy-start.10 = (bf16[1,1,256,256]{3,2,1,0:T(8,128)(2,1)S(1)}, bf16[1,1,256,256]{3,2,1,0:T(8,128)(2,1)}, u32[]{:S(2)}) copy-start(bf16[1,1,256,256]{3,2,1,0:T(8,128)(2,1)} %param.57) | copy-start | bytes 393220
  33.6 107.8 %copy-start.8 = (bf16[1,256,256]{2,1,0:T(8,128)(2,1)S(1)}, bf16[1,256,256]{2,1,0:T(8,128)(2,1)}, u32[]{:S(2)}) copy-start(bf16[1,256,256]{2,1,0:T(8,128)(2,1)} %param.51) | copy-start | bytes 393220
  33.6 109.6 %copy-start.9 = (bf16[1,256,256]{2,1,0:T(8,128)(2,1)S(1)}, bf16[1,256,256]{2,1,0:T(8,128)(2,1)}, u32[]{:S(2)}) copy-start(bf16[1,256,256]{2,1,0:T(8,128)(2,1)} %param.59) | copy-start | bytes 393220
  35.8 105.6 %all-reduce.25.cloned.1.call-start = ((), (), s32[]{:S(2)}) async-start(), calls=%async_computation.7 | async-start | bytes 524288 | tf_op jit(solution)/shard_map/psum | solution.py:125
  82.1 1.8 copy-start.15
  85.8 100.7 %all-reduce.13.cloned.1.call-start = ((), (), s32[]{:S(2)}) async-start(), calls=%async_computation.1 | async-start | bytes 262144 | tf_op jit(solution)/shard_map/psum | solution.py:127
  145.0 89.3 %all-reduce.15.cloned.1.call-start = ((), (), s32[]{:S(2)}) async-start(), calls=%async_computation.2 | async-start | bytes 262144 | tf_op jit(solution)/shard_map/psum | solution.py:139
  192.0 118.2 %all-reduce.17.cloned.1.call-start = ((), (), s32[]{:S(2)}) async-start(), calls=%async_computation.3 | async-start | bytes 262144 | tf_op jit(solution)/shard_map/psum | solution.py:120
  234.4 3.6 copy-start.12
  236.6 1.8 copy-start.6
  236.6 1.8 copy-start.43
  236.6 1.8 copy-start.52
  236.6 2.4 copy-start.3
  236.6 2.4 copy-start.62
  238.0 1.5 copy-start.68
  238.3 1.9 copy-start.39
  238.3 1.9 copy-start.46
  238.3 2.0 copy-start.60
  239.0 1.6 copy-start.19
  239.0 1.7 copy-start.37
  239.0 1.8 copy-start.58
  239.3 1.8 copy-start.35
  239.5 1.7 copy-start.64
  239.5 2.4 copy-start.32
  240.2 1.9 copy-start.66
  240.2 2.1 copy-start.30
  240.4 2.1 copy-start.20
  240.4 2.8 copy-start.27
  240.4 2.8 copy-start.56
  240.8 1.7 copy-start.21
  267.8 102.9 %all-reduce.23.cloned.1.call-start = ((), (), s32[]{:S(2)}) async-start(), calls=%async_computation.6 | async-start | bytes 524288 | tf_op jit(solution)/shard_map/psum | solution.py:125
  311.4 1.8 copy-start.14
  315.0 100.6 %all-reduce.19.cloned.1.call-start = ((), (), s32[]{:S(2)}) async-start(), calls=%async_computation.4 | async-start | bytes 262144 | tf_op jit(solution)/shard_map/psum | solution.py:127
  374.2 89.4 %all-reduce.21.cloned.1.call-start = ((), (), s32[]{:S(2)}) async-start(), calls=%async_computation.5 | async-start | bytes 262144 | tf_op jit(solution)/shard_map/psum | solution.py:139
  419.5 47.3 %copy-start.13 = (bf16[128,256]{1,0:T(8,128)(2,1)S(1)}, bf16[128,256]{1,0:T(8,128)(2,1)}, u32[]{:S(2)}) copy-start(bf16[128,256]{1,0:T(8,128)(2,1)} %convolution_convert_fusion.1) | copy-start | bytes 196612
  419.5 49.0 %copy-start.11 = (bf16[128,256]{1,0:T(8,128)(2,1)S(1)}, bf16[128,256]{1,0:T(8,128)(2,1)}, u32[]{:S(2)}) copy-start(bf16[128,256]{1,0:T(8,128)(2,1)} %convolution_convert_fusion.2) | copy-start | bytes 196612
  466.1 2.8 copy-start.44
  466.1 2.8 copy-start.53
  466.1 3.0 copy-start.63
  466.8 2.1 copy-start.7
  466.8 2.7 copy-start.4
  468.9 1.6 copy-start.61
  470.0 1.7 copy-start.33
  470.3 1.7 copy-start.28
  470.5 1.7 copy-start.57
  470.5 1.7 copy-start.70
  (23 other events, 25.2 us)
Sparse Core Ops, SparseCore 0:
  36.0 44.9 all-reduce.10
  85.9 55.5 all-reduce.24
  145.1 41.2 all-reduce.12
  192.1 42.2 all-reduce.14
  267.9 42.2 all-reduce.16
  315.1 55.5 all-reduce.22
  374.3 41.2 all-reduce.18
  421.3 42.2 all-reduce.20
where the time goes:
time: 484 us; the launch traced here: 482 us
  waiting for transfers between devices  328 us (68%)
  matrix products  94.3 us (19%)
  local copies, waits for them, and re-layouts  22.6 us (5%)
  blocking collectives  17.8 us (4%)
  between operations  16 us (3%)
    psum x2, waiting for transfers between devices, per_device(): strip_partial, summit_early = lax.psum((strip_term, summit_term), 'prow')  110 us
    dot_general x76, matrix products, multiply(): return jnp.einsum(form, left, right, preferred_element_type=jnp.float32)  94.3 us
    psum x2, waiting for transfers between devices, per_device(): lax.psum(summit_early + multiply(lift_strip, strip_solved, 'ki,kn->in'),...  81.6 us
    psum x2, waiting for transfers between devices, per_device(): band_partial = lax.psum(band_term, 'pcol')  76 us
    psum x2, waiting for transfers between devices, per_device(): lax.psum(downward, 'pcol')  60 us
    all_gather x2, blocking collectives, per_device(): lax.all_gather(band_piece, 'pcol', axis=0, tiled=True)  17.8 us
    unnamed x175, local copies, waits for them, and re-layouts  11.7 us
  transfers between devices with their start and end apart: 8, of which 8 were waited for; matrix products, arithmetic and copies ran while one was open for 4% of the time, Pallas kernels for 0%

commit v1 on v0

--- a/solution.py
+++ b/solution.py
@@ -117,7 +117,10 @@
         band_term = multiply(to_band, solved, "aij,ajr->ir")
         strip_term = multiply(to_strip, solved, "aij,ajr->ir")
         summit_term = multiply(to_summit, solved, "aij,ajr->ir")
-        band_partial = lax.psum(band_term, "pcol")
+        count, band_partial = (lax.axis_size("pcol"), band_term)
+        for far in [1 << k for k in range(count.bit_length() - 1)]:
+            swap = [(i, i ^ far) for i in range(count)]
+            band_partial = band_partial + lax.ppermute(band_partial, "pcol", swap)
         band_solved = forward_block(band_inverse[0], band_now, band_partial)
         own_band = lax.dynamic_slice_in_dim(band_solved, column_place, band_slab, 0)
         summit_term = summit_term + multiply(lift_band, own_band, "ki,kn->in")

time: 484 us -> 415 us (0.86)
  waiting for transfers between devices: 328 us -> 259 us
  matrix products: 94.3 us -> 84 us
  starting transfers between devices: 0.33 us -> 7.81 us
    psum x2 -> x0, waiting for transfers between devices: 76 us -> none  [per_device(): band_partial = lax.psum(band_term, 'pcol')]
    dot_general x76, matrix products: 94.3 us -> 84 us  [multiply(): return jnp.einsum(form, left, right, preferred_element_type=jnp.float32)]
    ppermute x0 -> x4, starting transfers between devices: none -> 7.57 us  [per_device(): band_partial = band_partial + lax.ppermute(band_partial, 'pcol', swap)]
    ppermute x0 -> x4, waiting for transfers between devices: none -> 7.01 us  [per_device(): band_partial = band_partial + lax.ppermute(band_partial, 'pcol', swap)]
    unnamed x175 -> x190, local copies, waits for them, and re-layouts: 11.7 us -> 13.2 us
  transfers between devices with their start and end apart: 8 -> 10, of which waited for: 8 -> 9; matrix products, arithmetic and copies ran while one was open for 4% -> 5% of each run, Pallas kernels for 0% -> 0%
where the time goes in v1:
time: 415 us; the launch traced here: 413 us
  waiting for transfers between devices  259 us (62%)
  matrix products  84 us (20%)
  local copies, waits for them, and re-layouts  23.7 us (6%)
  blocking collectives  17.8 us (4%)
  between operations  16 us (4%)
  starting transfers between devices  7.81 us (2%)
  other arithmetic  4.49 us (1%)
    psum x2, waiting for transfers between devices, per_device(): strip_partial, summit_early = lax.psum((strip_term, summit_term), 'prow')  110 us
    dot_general x76, matrix products, multiply(): return jnp.einsum(form, left, right, preferred_element_type=jnp.float32)  84 us
    psum x2, waiting for transfers between devices, per_device(): lax.psum(summit_early + multiply(lift_strip, strip_solved, 'ki,kn->in'),...  81.6 us
    psum x2, waiting for transfers between devices, per_device(): lax.psum(downward, 'pcol')  60 us
    all_gather x2, blocking collectives, per_device(): lax.all_gather(band_piece, 'pcol', axis=0, tiled=True)  17.8 us
    unnamed x190, local copies, waits for them, and re-layouts  13.2 us
  transfers between devices with their start and end apart: 10, of which 9 were waited for; matrix products, arithmetic and copies ran while one was open for 5% of the time, Pallas kernels for 0%

profile of v1, /device:TPU:0, one launch (start us, length us, event | category | flops | bytes accessed | tf_op | source)
XLA Modules:
  0.0 413.0 jit_solution(5174131508977596106)
XLA Ops:
  12.0 1.1 fusion.587
  13.8 1.9 constant_dynamic-update-slice_fusion.17
  15.7 2.0 constant_dynamic-update-slice_fusion.16
  17.7 2.1 constant_dynamic-update-slice_fusion.15
  19.7 2.1 constant_dynamic-update-slice_fusion.14
  21.8 2.2 constant_dynamic-update-slice_fusion.13
  25.0 2.5 constant_dynamic-update-slice_fusion.12
  28.3 2.6 constant_dynamic-update-slice_fusion.11
  30.9 2.6 constant_dynamic-update-slice_fusion.18
  33.5 2.2 convolution_bitcast_fusion.21
  35.7 3.0 collective-permute-start
  38.7 1.2 slice_bitcast_fusion.14
  39.9 1.2 slice_bitcast_fusion.15
  41.1 1.2 slice_bitcast_fusion.16
  42.3 1.2 slice_bitcast_fusion.17
  43.4 1.6 copy.33
  45.0 1.5 convolution_bitcast_fusion.19
  47.5 1.6 collective-permute-start.1
  49.1 1.5 convolution_bitcast_fusion.20
  50.6 2.0 collective-permute-done.1
  54.6 1.2 slice_bitcast_fusion.18
  55.8 54.7 %all-reduce.19.cloned.1.call-done = (f32[256,128]{1,0:T(8,128)}, f32[256,128]{1,0:T(8,128)}) async-done(((f32[256,128]{1,0:T(8,128)}, f32[256,128]{1,0:T(8,128)}), (f32[256,128]{1,0:T(8,128)}, f32[256,128]{1,0:T(8,128)})) %all-reduce.19.cloned.1.call-update) | async-done | bytes 262160 | tf_op jit(solution)/shard_map/psum | solution.py:128
  110.6 1.1 convolution_convert_fusion.10
  112.3 1.8 fusion.30
  114.2 1.2 slice_bitcast_fusion.19
  115.3 40.2 %all-reduce.9.cloned.1.call-done = f32[256,128]{1,0:T(8,128)} async-done(((f32[256,128]{1,0:T(8,128)}), f32[256,128]{1,0:T(8,128)}) %all-reduce.9.cloned.1.call-update) | async-done | bytes 131088 | tf_op jit(solution)/shard_map/psum | solution.py:130
  155.5 2.0 convolution_convert_fusion.8
  157.5 1.8 convolution_convert_fusion.7
  159.4 1.7 convolution_bitcast_fusion.11
  162.1 9.1 %all_gather.6 = f32[256,128]{1,0:T(8,128)} all-gather(f32[64,128]{1,0:T(8,128)S(1)} %convolution_bitcast_fusion.24), channel_id=1, replica_groups=mesh['prow'=8,'pcol'=4] {'pcol'}, dimensions={0}, use_global_device_ids=true | all-gather | bytes 163840 | tf_op jit(solution)/shard_map/all_gather | solution.py:142
  171.1 1.7 copy.41
  172.8 30.6 %all-reduce.11.cloned.1.call-done = f32[256,128]{0,1:T(8,128)} async-done(((f32[256,128]{0,1:T(8,128)}), f32[256,128]{0,1:T(8,128)}) %all-reduce.11.cloned.1.call-update) | async-done | bytes 131088 | tf_op jit(solution)/shard_map/psum | solution.py:142
  203.4 1.2 convolution_convert_fusion.6
  205.7 1.3 convolution_add_fusion.3
  212.2 1.4 fusion.79
  213.5 2.0 constant_dynamic-update-slice_fusion.43
  215.5 2.1 constant_dynamic-update-slice_fusion.42
  217.6 2.2 constant_dynamic-update-slice_fusion.41
  219.8 2.3 constant_dynamic-update-slice_fusion.40
  222.2 2.4 constant_dynamic-update-slice_fusion.39
  224.5 2.5 constant_dynamic-update-slice_fusion.38
  227.0 2.6 constant_dynamic-update-slice_fusion.37
  229.7 2.7 constant_dynamic-update-slice_fusion.44
  232.4 1.6 convolution_bitcast_fusion.17
  234.0 1.5 collective-permute-start.2
  235.5 1.5 convolution_bitcast_fusion.15
  237.0 2.0 collective-permute-done.2
  239.0 1.5 collective-permute-start.3
  241.0 3.1 collective-permute-done.3
  246.1 55.6 %all-reduce.17.cloned.1.call-done = (f32[256,128]{0,1:T(8,128)}, f32[256,128]{0,1:T(8,128)}) async-done(((f32[256,128]{0,1:T(8,128)}, f32[256,128]{0,1:T(8,128)}), (f32[256,128]{0,1:T(8,128)}, f32[256,128]{0,1:T(8,128)})) %all-reduce.17.cloned.1.call-update) | async-done | bytes 262160 | tf_op jit(solution)/shard_map/psum | solution.py:128
  301.7 1.1 convolution_convert_fusion.4
  303.4 1.7 fusion.27
  305.2 41.4 %all-reduce.13.cloned.1.call-done = f32[256,128]{0,1:T(8,128)} async-done(((f32[256,128]{0,1:T(8,128)}), f32[256,128]{0,1:T(8,128)}) %all-reduce.13.cloned.1.call-update) | async-done | bytes 131088 | tf_op jit(solution)/shard_map/psum | solution.py:130
  346.6 2.0 convolution_convert_fusion.2
  348.6 1.8 convolution_convert_fusion.1
  350.5 1.7 convolution_bitcast_fusion.8
  353.2 1.6 copy.46
  354.8 1.6 copy.45
  356.4 8.8 %all_gather.7 = f32[256,128]{1,0:T(8,128)S(1)} all-gather(f32[64,128]{1,0:T(8,128)S(1)} %convolution_bitcast_fusion.23), channel_id=1, replica_groups=mesh['prow'=8,'pcol'=4] {'pcol'}, dimensions={0}, use_global_device_ids=true | all-gather | bytes 163840 | tf_op jit(solution)/shard_map/all_gather | solution.py:142
  365.2 29.4 %all-reduce.15.cloned.1.call-done = f32[256,128]{0,1:T(8,128)} async-done(((f32[256,128]{0,1:T(8,128)}), f32[256,128]{0,1:T(8,128)}) %all-reduce.15.cloned.1.call-update) | async-done | bytes 131088 | tf_op jit(solution)/shard_map/psum | solution.py:142
  394.6 1.2 convolution_convert_fusion
  395.7 1.3 fusion.132
  397.8 1.7 convolution_add_fusion.1
  403.2 1.8 fusion.123
  (260 shorter events, 26.4 us)
Async XLA Ops:
  7.2 26.3 %copy-start = (bf16[1,1,8,256,256]{4,3,2,1,0:T(8,128)(2,1)S(1)}, bf16[1,1,8,256,256]{4,3,2,1,0:T(8,128)(2,1)}, u32[]{:S(2)}) copy-start(bf16[1,1,8,256,256]{4,3,2,1,0:T(8,128)(2,1)} %param.54) | copy-start | bytes 3145732
  7.2 103.4 %all-reduce.19.cloned.1.call-start = ((), (), s32[]{:S(2)}) async-start(), calls=%async_computation.5 | async-start | bytes 524288 | tf_op jit(solution)/shard_map/psum | solution.py:128
  10.5 20.4 %copy-start.80 = (bf16[7]{0:T(256)(128)(2,1)}, bf16[7]{0:T(256)(128)(2,1)S(1)}, u32[]{:S(2)}) copy-start(bf16[7]{0:T(256)(128)(2,1)S(1)} %fusion.586) | copy-start | bytes 46
  10.5 17.7 %copy-start.81 = (bf16[6]{0:T(256)(128)(2,1)}, bf16[6]{0:T(256)(128)(2,1)S(1)}, u32[]{:S(2)}) copy-start(bf16[6]{0:T(256)(128)(2,1)S(1)} %fusion.585) | copy-start | bytes 40
  10.5 14.4 %copy-start.82 = (bf16[5]{0:T(256)(128)(2,1)}, bf16[5]{0:T(256)(128)(2,1)S(1)}, u32[]{:S(2)}) copy-start(bf16[5]{0:T(256)(128)(2,1)S(1)} %fusion.584) | copy-start | bytes 34
  10.6 13.5 %copy-start.83 = (bf16[4]{0:T(256)(128)(2,1)}, bf16[4]{0:T(256)(128)(2,1)S(1)}, u32[]{:S(2)}) copy-start(bf16[4]{0:T(256)(128)(2,1)S(1)} %fusion.583) | copy-start | bytes 28
  10.6 13.5 %copy-start.84 = (bf16[3]{0:T(256)(128)(2,1)}, bf16[3]{0:T(256)(128)(2,1)S(1)}, u32[]{:S(2)}) copy-start(bf16[3]{0:T(256)(128)(2,1)S(1)} %fusion.582) | copy-start | bytes 22
  10.6 13.5 %copy-start.85 = (bf16[2]{0:T(256)(128)(2,1)}, bf16[2]{0:T(256)(128)(2,1)S(1)}, u32[]{:S(2)}) copy-start(bf16[2]{0:T(256)(128)(2,1)S(1)} %fusion.581) | copy-start | bytes 16
  11.9 12.1 %copy-start.62 = (f32[1,256]{1,0:T(1,128)}, f32[1,256]{1,0:T(1,128)S(1)}, u32[]{:S(2)}) copy-start(f32[1,256]{1,0:T(1,128)S(1)} %get-tuple-element.248) | copy-start | bytes 3076
  11.9 13.0 %copy-start.52 = (f32[1,256]{1,0:T(1,128)}, f32[1,256]{1,0:T(1,128)S(1)}, u32[]{:S(2)}) copy-start(f32[1,256]{1,0:T(1,128)S(1)} %get-tuple-element.243) | copy-start | bytes 3076
  12.0 16.3 %copy-start.55 = (f32[1,256]{1,0:T(1,128)}, f32[1,256]{1,0:T(1,128)S(1)}, u32[]{:S(2)}) copy-start(f32[1,256]{1,0:T(1,128)S(1)} %get-tuple-element.242) | copy-start | bytes 3076
  12.0 18.9 %copy-start.58 = (f32[1,256]{1,0:T(1,128)}, f32[1,256]{1,0:T(1,128)S(1)}, u32[]{:S(2)}) copy-start(f32[1,256]{1,0:T(1,128)S(1)} %get-tuple-element.241) | copy-start | bytes 3076
  15.7 11.8 %copy-start.33 = (bf16[128,256]{1,0:T(8,128)(2,1)}, bf16[128,256]{1,0:T(8,128)(2,1)S(1)}, u32[]{:S(2)}) copy-start(bf16[128,256]{1,0:T(8,128)(2,1)S(1)} %get-tuple-element.249) | copy-start | bytes 196612
  17.7 9.8 %copy-start.36 = (bf16[128,256]{1,0:T(8,128)(2,1)}, bf16[128,256]{1,0:T(8,128)(2,1)S(1)}, u32[]{:S(2)}) copy-start(bf16[128,256]{1,0:T(8,128)(2,1)S(1)} %get-tuple-element.250) | copy-start | bytes 196612
  19.7 7.8 %copy-start.38 = (bf16[128,256]{1,0:T(8,128)(2,1)}, bf16[128,256]{1,0:T(8,128)(2,1)S(1)}, u32[]{:S(2)}) copy-start(bf16[128,256]{1,0:T(8,128)(2,1)S(1)} %get-tuple-element.251) | copy-start | bytes 196612
  21.8 5.7 %copy-start.41 = (bf16[128,256]{1,0:T(8,128)(2,1)}, bf16[128,256]{1,0:T(8,128)(2,1)S(1)}, u32[]{:S(2)}) copy-start(bf16[128,256]{1,0:T(8,128)(2,1)S(1)} %get-tuple-element.252) | copy-start | bytes 196612
  25.0 20.0 %copy-start.2 = (bf16[1,1,8,256,256]{4,3,2,1,0:T(8,128)(2,1)S(1)}, bf16[1,1,8,256,256]{4,3,2,1,0:T(8,128)(2,1)}, u32[]{:S(2)}) copy-start(bf16[1,1,8,256,256]{4,3,2,1,0:T(8,128)(2,1)} %param.56) | copy-start | bytes 3145732
  28.3 20.8 %copy-start.1 = (bf16[1,1,8,256,256]{4,3,2,1,0:T(8,128)(2,1)S(1)}, bf16[1,1,8,256,256]{4,3,2,1,0:T(8,128)(2,1)}, u32[]{:S(2)}) copy-start(bf16[1,1,8,256,256]{4,3,2,1,0:T(8,128)(2,1)} %param.55) | copy-start | bytes 3145732
  30.9 21.9 %copy-start.11 = (bf16[1,1,256,256]{3,2,1,0:T(8,128)(2,1)S(1)}, bf16[1,1,256,256]{3,2,1,0:T(8,128)(2,1)}, u32[]{:S(2)}) copy-start(bf16[1,1,256,256]{3,2,1,0:T(8,128)(2,1)} %param.57) | copy-start | bytes 393220
  33.5 77.1 %copy-start.9 = (bf16[1,256,256]{2,1,0:T(8,128)(2,1)S(1)}, bf16[1,256,256]{2,1,0:T(8,128)(2,1)}, u32[]{:S(2)}) copy-start(bf16[1,256,256]{2,1,0:T(8,128)(2,1)} %param.51) | copy-start | bytes 393220
  33.5 78.8 %copy-start.10 = (bf16[1,256,256]{2,1,0:T(8,128)(2,1)S(1)}, bf16[1,256,256]{2,1,0:T(8,128)(2,1)}, u32[]{:S(2)}) copy-start(bf16[1,256,256]{2,1,0:T(8,128)(2,1)} %param.59) | copy-start | bytes 393220
  35.7 10.8 %collective-permute-start = (f32[256,128]{0,1:T(8,128)}, f32[256,128]{0,1:T(8,128)}, u32[]{:S(2)}, u32[]{:S(2)}) collective-permute-start(f32[256,128]{0,1:T(8,128)} %convolution_bitcast_fusion.21), channel_id=1, source_target_pairs={{0,1},{1,0},{2,3},{3,2},{4,5},{5,4},{6,7},{7,6},{8,9},{9,8},{10,11... | collective-permute-start | bytes 393224 | tf_op jit(solution)/shard_map/ppermute | solution.py:123
  45.0 7.6 %copy-start.12 = (bf16[1,256,256]{2,1,0:T(8,128)(2,1)S(1)}, bf16[1,256,256]{2,1,0:T(8,128)(2,1)}, u32[]{:S(2)}) copy-start(bf16[1,256,256]{2,1,0:T(8,128)(2,1)} %param.50) | copy-start | bytes 393220
  45.0 7.6 %copy-start.31 = (bf16[1,256,128]{1,2,0:T(8,128)(2,1)S(1)}, bf16[1,256,128]{1,2,0:T(8,128)(2,1)}, u32[]{:S(2)}) copy-start(bf16[1,256,128]{1,2,0:T(8,128)(2,1)} %copy.33) | copy-start | bytes 196612
  45.0 8.6 %copy-start.23 = (bf16[1,64,256]{2,1,0:T(8,128)(2,1)S(1)}, bf16[1,64,256]{2,1,0:T(8,128)(2,1)}, u32[]{:S(2)}) copy-start(bf16[1,64,256]{2,1,0:T(8,128)(2,1)} %param.58) | copy-start | bytes 98308
  47.5 5.0 %collective-permute-start.1 = (f32[256,128]{0,1:T(8,128)S(1)}, f32[256,128]{0,1:T(8,128)S(1)}, u32[]{:S(2)}, u32[]{:S(2)}) collective-permute-start(f32[256,128]{0,1:T(8,128)S(1)} %add.186), channel_id=1, source_target_pairs={{0,2},{1,3},{2,0},{3,1},{4,6},{5,7},{6,4},{7,5},{8,10},{9,11},{10,... | collective-permute-start | bytes 393224 | tf_op jit(solution)/shard_map/ppermute | solution.py:123
  54.6 101.0 %all-reduce.9.cloned.1.call-start = ((), (), s32[]{:S(2)}) async-start(), calls=%async_computation | async-start | bytes 262144 | tf_op jit(solution)/shard_map/psum | solution.py:130
  114.1 89.3 %all-reduce.11.cloned.1.call-start = ((), (), s32[]{:S(2)}) async-start(), calls=%async_computation.1 | async-start | bytes 262144 | tf_op jit(solution)/shard_map/psum | solution.py:142
  161.0 140.7 %all-reduce.17.cloned.1.call-start = ((), (), s32[]{:S(2)}) async-start(), calls=%async_computation.4 | async-start | bytes 524288 | tf_op jit(solution)/shard_map/psum | solution.py:128
  203.4 3.6 copy-start.15
  205.6 1.8 copy-start.7
  205.6 1.8 copy-start.49
  205.6 1.8 copy-start.59
  205.6 2.4 copy-start.3
  205.7 2.4 copy-start.69
  207.3 1.8 copy-start.46
  207.4 1.8 copy-start.53
  207.4 2.0 copy-start.67
  208.1 1.8 copy-start.65
  208.4 1.8 copy-start.42
  208.6 1.7 copy-start.71
  208.6 2.3 copy-start.39
  209.2 1.9 copy-start.73
  209.2 2.1 copy-start.37
  209.4 2.1 copy-start.26
  209.4 2.8 copy-start.34
  209.4 2.8 copy-start.63
  232.3 8.1 %copy-start.5 = (bf16[8,256,128]{1,2,0:T(8,128)(2,1)S(1)}, bf16[8,256,128]{1,2,0:T(8,128)(2,1)}, u32[]{:S(2)}) copy-start(bf16[8,256,128]{1,2,0:T(8,128)(2,1)} %get-tuple-element.265) | copy-start | bytes 1572868
  232.3 11.7 %copy-start.13 = (bf16[1,256,256]{2,1,0:T(8,128)(2,1)S(1)}, bf16[1,256,256]{2,1,0:T(8,128)(2,1)}, u32[]{:S(2)}) copy-start(bf16[1,256,256]{2,1,0:T(8,128)(2,1)} %param.50) | copy-start | bytes 393220
  232.3 11.7 %copy-start.22 = (bf16[128,256]{1,0:T(8,128)(2,1)S(1)}, bf16[128,256]{1,0:T(8,128)(2,1)}, u32[]{:S(2)}) copy-start(bf16[128,256]{1,0:T(8,128)(2,1)} %copy-done.21) | copy-start | bytes 196612
  232.3 11.9 %copy-start.24 = (bf16[1,64,256]{2,1,0:T(8,128)(2,1)S(1)}, bf16[1,64,256]{2,1,0:T(8,128)(2,1)}, u32[]{:S(2)}) copy-start(bf16[1,64,256]{2,1,0:T(8,128)(2,1)} %param.58) | copy-start | bytes 98308
  234.0 5.0 %collective-permute-start.2 = (f32[256,128]{0,1:T(8,128)S(1)}, f32[256,128]{0,1:T(8,128)S(1)}, u32[]{:S(2)}, u32[]{:S(2)}) collective-permute-start(f32[256,128]{0,1:T(8,128)S(1)} %convolution_bitcast_fusion.17), channel_id=1, source_target_pairs={{0,1},{1,0},{2,3},{3,2},{4,5},{5,4},{6,7},{7,6},{8,9},{9,8},{10,11... | collective-permute-start | bytes 393224 | tf_op jit(solution)/shard_map/ppermute | solution.py:123
  239.0 5.0 %collective-permute-start.3 = (f32[256,128]{0,1:T(8,128)S(1)}, f32[256,128]{0,1:T(8,128)S(1)}, u32[]{:S(2)}, u32[]{:S(2)}) collective-permute-start(f32[256,128]{0,1:T(8,128)S(1)} %add.205), channel_id=1, source_target_pairs={{0,2},{1,3},{2,0},{3,1},{4,6},{5,7},{6,4},{7,5},{8,10},{9,11},{10,... | collective-permute-start | bytes 393224 | tf_op jit(solution)/shard_map/ppermute | solution.py:123
  246.0 100.6 %all-reduce.13.cloned.1.call-start = ((), (), s32[]{:S(2)}) async-start(), calls=%async_computation.2 | async-start | bytes 262144 | tf_op jit(solution)/shard_map/psum | solution.py:130
  305.2 89.4 %all-reduce.15.cloned.1.call-start = ((), (), s32[]{:S(2)}) async-start(), calls=%async_computation.3 | async-start | bytes 262144 | tf_op jit(solution)/shard_map/psum | solution.py:142
  350.5 47.3 %copy-start.16 = (bf16[128,256]{1,0:T(8,128)(2,1)S(1)}, bf16[128,256]{1,0:T(8,128)(2,1)}, u32[]{:S(2)}) copy-start(bf16[128,256]{1,0:T(8,128)(2,1)} %convolution_convert_fusion.1) | copy-start | bytes 196612
  350.5 49.0 %copy-start.14 = (bf16[128,256]{1,0:T(8,128)(2,1)S(1)}, bf16[128,256]{1,0:T(8,128)(2,1)}, u32[]{:S(2)}) copy-start(bf16[128,256]{1,0:T(8,128)(2,1)} %convolution_convert_fusion.2) | copy-start | bytes 196612
  397.0 2.8 copy-start.51
  397.0 2.8 copy-start.60
  397.0 3.0 copy-start.70
  397.7 2.1 copy-start.8
  397.8 2.7 copy-start.4
  401.3 1.7 copy-start.35
  401.5 1.7 copy-start.64
  (32 other events, 38.2 us)
Sparse Core Ops, SparseCore 0:
  54.7 55.8 all-reduce.18
  114.2 41.2 all-reduce.8
  161.2 42.2 all-reduce.10
  246.1 55.5 all-reduce.16
  305.3 41.2 all-reduce.12
  352.3 42.2 all-reduce.14
